TPU v7x, 32 devices: a whole 2x2x4 slice. The times are simulated.
32 devices in a mesh: row: 4 (over z), col: 8 (over y, x, core).
Axes of the slice: x: 2, y: 2, z: 4, core: 2. Of those that a mesh axis runs over, the one named last changes fastest.
Arguments:
- pair_products: bfloat16 [32, 64, 64, 64], P(('row', 'col')), may hold values from -6 to 6
- pw_index: int32 [8192], replicated, may hold values from 4096 to 131071, as said below
- valence_band: int32 [32], replicated, may hold values from 0 to 2047
- conduction_band: int32 [32], replicated, may hold values from 0 to 2047
- valence_energy: float32 [2048], replicated, may hold values from -10 to -0.5
- conduction_energy: float32 [2048], replicated, may hold values from 0.5 to 10
- imag_freq: float32 [2], replicated, may hold values from 0.3 to 12
Outputs:
- chi0: float32 [2, 16384, 16384], P(None, 'row', 'col')
Inputs may be any that keep to these rules, and one draw needn't show every extreme that they name: `pw_index`: distinct flat indices (first grid index slowest) of grid points whose first component lies in 1 to 31, so no G-vector is zero and none is the negative of another.
All inputs are finite; a program needn't handle non-finite values.
Results may differ from a plain program's by a relative error of at most 0.0048.
Values may be sent and summed in bfloat16 or wider, within the bound.
A program may use at most 128 MiB of HBM per device.

v0:
```python
import math

import jax
import jax.numpy as jnp
from jax import lax
from jax.sharding import PartitionSpec as P

HIGHER = lax.Precision.HIGH


def transform(pair_products, pw_index):
    points = pair_products.shape[1]
    upper = points // 2
    counter = jnp.arange(points, dtype=jnp.int32)
    phases = counter[:, None] * counter[None, :] % points
    angles = phases.astype(jnp.float32) * (2.0 * math.pi / points)
    cosine = jnp.cos(angles)
    sine = jnp.sin(angles)
    stacked = jnp.concatenate([cosine, -sine], axis=1)
    first = jnp.einsum(
        "pabc,cz->pabz",
        pair_products,
        stacked,
        precision=HIGHER,
        preferred_element_type=jnp.float32,
    )
    real_part = first[..., :points]
    imag_part = first[..., points:]
    next_real = jnp.einsum("pabc,bk->pakc", real_part, cosine, precision=HIGHER) + jnp.einsum(
        "pabc,bk->pakc", imag_part, sine, precision=HIGHER
    )
    next_imag = jnp.einsum("pabc,bk->pakc", imag_part, cosine, precision=HIGHER) - jnp.einsum(
        "pabc,bk->pakc", real_part, sine, precision=HIGHER
    )
    cos_part = cosine[:, 1:upper]
    sin_part = sine[:, 1:upper]
    final_real = jnp.einsum("pabc,ak->pkbc", next_real, cos_part, precision=HIGHER) + jnp.einsum(
        "pabc,ak->pkbc", next_imag, sin_part, precision=HIGHER
    )
    final_imag = jnp.einsum("pabc,ak->pkbc", next_imag, cos_part, precision=HIGHER) - jnp.einsum(
        "pabc,ak->pkbc", next_real, sin_part, precision=HIGHER
    )
    count_pairs = pair_products.shape[0]
    shifted = pw_index - jnp.int32(points * points)
    flat_real = jnp.take(final_real.reshape(count_pairs, -1), shifted, axis=1)
    flat_imag = jnp.take(final_imag.reshape(count_pairs, -1), shifted, axis=1)
    scale = float(points) ** (-1.5)
    return (jnp.concatenate([flat_real, -flat_imag], axis=1) * scale).astype(jnp.bfloat16)


def lookup(indices, table):
    slots = jnp.arange(table.shape[0], dtype=jnp.int32)
    return jnp.sum(jnp.where(indices[:, None] == slots[None, :], table[None, :], 0.0), axis=1)


def pair_weights(valence_band, conduction_band, valence_energy, conduction_energy, imag_freq):
    gap = lookup(conduction_band, conduction_energy) - lookup(valence_band, valence_energy)
    total = valence_band.shape[0]
    return (
        -4.0
        * gap[:, None]
        / (gap[:, None] ** 2 + imag_freq[None, :] ** 2)
        / jnp.sqrt(jnp.float32(total))
    )


def shards(
    pair_products,
    pw_index,
    valence_band,
    conduction_band,
    valence_energy,
    conduction_energy,
    imag_freq,
):
    coefficients = transform(pair_products, pw_index)
    pair_count = coefficients.shape[0]
    blocks = lax.all_to_all(coefficients, "col", split_axis=1, concat_axis=0, tiled=True)
    column_panel = lax.all_gather(blocks, "row", axis=0, tiled=True)
    total_pairs = column_panel.shape[0]
    col_width = column_panel.shape[1]
    weights = pair_weights(
        valence_band, conduction_band, valence_energy, conduction_energy, imag_freq
    )
    freq_count = weights.shape[1]
    weighted = (column_panel.astype(jnp.float32)[:, None, :] * weights[:, :, None]).astype(
        jnp.bfloat16
    )
    weighted = weighted.reshape(total_pairs, freq_count * col_width)
    row_count = lax.axis_size("row")
    col_count = lax.axis_size("col")
    contract = (((0,), (0,)), ((), ()))
    row_blocks = lax.all_to_all(coefficients, "row", split_axis=1, concat_axis=0, tiled=True)
    row_width = row_blocks.shape[1]
    permuted = (
        weighted.reshape(row_count, col_count, pair_count, -1)
        .transpose(1, 0, 2, 3)
        .reshape(total_pairs, -1)
    )
    row_panel = lax.all_gather(row_blocks, "col", axis=0, tiled=True)
    chi_tile = lax.dot_general(row_panel, permuted, contract, preferred_element_type=jnp.float32)
    return chi_tile.reshape(row_width, freq_count, col_width).transpose(1, 0, 2)


def solution(mesh):
    in_specs = (P(("row", "col"), None, None, None), P(), P(), P(), P(), P(), P())
    out_specs = P(None, "row", "col")
    return jax.shard_map(shards, mesh=mesh, in_specs=in_specs, out_specs=out_specs, check_vma=False)
```

profile of v0, /device:TPU:0, one launch (start us, length us, event | category | flops | bytes accessed | tf_op | source)
XLA Modules:
  0.0 177.4 jit_solution(15805326162453613646)
XLA Ops:
  0.0 0.0 copy-start
  0.0 0.1 fusion.38
  0.1 0.1 fusion.39
  0.3 0.9 copy-done
  1.2 0.8 convolution_bitcast_fusion.1
  2.0 1.2 fusion
  3.2 0.0 copy-start.1
  3.2 1.2 fusion.1
  4.5 0.0 copy-done.1
  4.5 1.6 subtract_bitcast_fusion
  6.1 1.8 %fusion.4 = f32[31,64,64]{2,0,1:T(8,128)S(1)} fusion(f32[64,64,64]{2,1,0:T(8,128)S(1)} %subtract_bitcast_fusion, f32[64,64]{1,0:T(8,128)S(1)} %get-tuple-element.12), kind=kOutput, calls=%fused_computation.11 | convolution fusion | flops 48758784 | bytes 1572864 | tf_op jit(solution)/shard_map/pabc,ak->pkbc/dot_general | solution.py:40
  8.0 1.8 %fusion.6 = f32[31,64,64]{2,0,1:T(8,128)S(1)} fusion(f32[64,64,64]{2,1,0:T(8,128)S(1)} %subtract_bitcast_fusion, f32[64,64]{1,0:T(8,128)S(1)} %fusion.38), kind=kOutput, calls=%fused_computation.13 | convolution fusion | flops 48758784 | bytes 1572864 | tf_op jit(solution)/shard_map/pabc,ak->pkbc/dot_general | solution.py:37
  9.8 1.6 add_bitcast_fusion
  11.5 1.9 %fusion.15 = f32[31,64,64]{2,0,1:T(8,128)S(1)} fusion(f32[31,64,64]{2,0,1:T(8,128)S(1)} %fusion.4, f32[64,64,64]{2,1,0:T(8,128)S(1)} %add_bitcast_fusion, f32[64,64]{1,0:T(8,128)S(1)} %fusion.38), kind=kOutput, calls=%fused_computation.21 | convolution fusion | flops 48885760 | bytes 2080768 | tf_op jit(solution)/shard_map/pabc,ak->pkbc/dot_general | solution.py:40
  13.3 2.0 %fusion.12 = f32[31,64,64]{2,0,1:T(8,128)S(1)} fusion(f32[31,64,64]{2,0,1:T(8,128)S(1)} %fusion.6, f32[64,64,64]{2,1,0:T(8,128)S(1)} %add_bitcast_fusion, f32[64,64]{1,0:T(8,128)S(1)} %get-tuple-element.12), kind=kOutput, calls=%fused_computation.20 | convolution fusion | flops 48885760 | bytes 2080768 | tf_op jit(solution)/shard_map/pabc,ak->pkbc/dot_general | solution.py:37
  15.4 1.5 copy.125
  16.9 1.4 reshape.269
  18.3 1.5 copy.130
  19.9 1.4 reshape.272
  21.3 45.5 %gather_fusion = f32[8192]{0:T(1024)S(1)} fusion(f32[126976]{0:T(1024)S(1)} %reshape.269, s32[8192]{0:T(1024)S(1)} %fusion.37), kind=kCustom, calls=%fused_computation.clone | custom fusion | bytes 98304 | tf_op jit(solution)/shard_map/jit(_take)/gather | solution.py:45
  66.8 0.0 copy-start.6
  66.8 0.0 copy-start.2
  66.9 0.0 copy-start.3
  66.9 0.0 copy-start.4
  66.9 0.0 copy-start.5
  66.9 45.5 %gather_fusion.1 = f32[8192]{0:T(1024)S(1)} fusion(f32[126976]{0:T(1024)S(1)} %reshape.272, s32[8192]{0:T(1024)S(1)} %fusion.37), kind=kCustom, calls=%fused_computation.1.clone | custom fusion | bytes 98304 | tf_op jit(solution)/shard_map/jit(_take)/gather | solution.py:46
  112.5 0.1 fusion.62
  112.6 0.5 broadcast.113
  113.1 0.8 reduce
  113.9 0.6 reshape.288
  114.6 5.2 %all-to-all-start.1 = ((bf16[8,2,1024]{2,1,0:T(2,128)(2,1)}), bf16[8,2,1024]{2,1,0:T(2,128)(2,1)S(1)}, u32[]{:S(2)}, u32[]{:S(2)}) async-start(bf16[8,2,1024]{2,1,0:T(2,128)(2,1)} %reshape.288), calls=%async_computation.1 | async-start | bytes 65536 | tf_op jit(solution)/shard_map/all_to_all | solution.py:78
  119.8 0.0 copy-done.6
  119.8 0.0 copy-done.2
  119.8 0.0 copy-done.3
  119.8 0.0 copy-done.4
  119.8 0.0 copy-done.5
  119.8 0.2 select_reduce_fusion
  120.1 0.1 fusion.63
  120.2 0.1 divide_multiply_fusion
  120.2 0.1 copy.132
  120.3 0.8 reduce.1
  121.1 0.6 reshape.290
  121.8 2.9 %all-to-all-done.1 = bf16[8,2,1024]{2,1,0:T(2,128)(2,1)S(1)} async-done(((bf16[8,2,1024]{2,1,0:T(2,128)(2,1)}), bf16[8,2,1024]{2,1,0:T(2,128)(2,1)S(1)}, u32[]{:S(2)}, u32[]{:S(2)}) %all-to-all-start.1) | async-done | bytes 32800 | tf_op jit(solution)/shard_map/all_to_all | solution.py:78
  124.6 4.9 %all-to-all-start = ((bf16[4,2,2048]{2,1,0:T(2,128)(2,1)}), bf16[4,2,2048]{2,1,0:T(2,128)(2,1)S(1)}, u32[]{:S(2)}, u32[]{:S(2)}) async-start(bf16[4,2,2048]{2,1,0:T(2,128)(2,1)} %reshape.290), calls=%async_computation | async-start | bytes 65536 | tf_op jit(solution)/shard_map/all_to_all | solution.py:93
  129.5 13.9 %all-gather.1 = bf16[1,32,2048]{2,1,0:T(8,128)(2,1)S(1)} all-gather(bf16[1,8,2048]{2,1,0:T(8,128)(2,1)S(1)} %copy.131), channel_id=3, replica_groups=mesh['row'=4,'col'=8] {'row'}, dimensions={1}, use_global_device_ids=true | all-gather | bytes 163840 | tf_op jit(solution)/shard_map/all_gather | solution.py:79
  143.5 0.2 multiply_convert_fusion
  143.7 0.2 convert_element_type.63
  143.9 0.2 copy.133
  144.1 0.1 reshape.241
  144.2 0.0 all-to-all-done
  144.2 9.0 %all-gather = bf16[1,32,4096]{2,0,1:T(2,128)(2,1)S(1)} all-gather(bf16[1,4,4096]{2,0,1:T(2,128)(2,1)S(1)} %bitcast.92), channel_id=2, replica_groups=mesh['row'=4,'col'=8] {'col'}, dimensions={1}, use_global_device_ids=true | all-gather | bytes 294912 | tf_op jit(solution)/shard_map/all_gather | solution.py:100
  153.3 24.2 %convolution_bitcast_fusion = f32[2,4096,2048]{2,1,0:T(8,128)} fusion(bf16[4,2,8,2048]{3,2,1,0:T(8,128)(2,1)S(1)} %bitcast.86, bf16[1,32,4096]{2,0,1:T(2,128)(2,1)S(1)} %all-gather), kind=kOutput, calls=%fused_computation.2 | convolution fusion | flops 1073741824 | bytes 67633152 | tf_op jit(solution)/shard_map/dot_general | solution.py:101
  (10 shorter events, 0.2 us)
Async XLA Ops:
  0.0 1.2 copy-start
  3.2 1.2 copy-start.1
  66.8 52.9 %copy-start.6 = (f32[2]{0:T(128)S(1)}, f32[2]{0:T(128)}, u32[]{:S(2)}) copy-start(f32[2]{0:T(128)} %param.15) | copy-start | bytes 28
  66.8 52.9 %copy-start.2 = (f32[2048]{0:T(1024)S(1)}, f32[2048]{0:T(1024)}, u32[]{:S(2)}) copy-start(f32[2048]{0:T(1024)} %param.13) | copy-start | bytes 24580
  66.9 52.9 %copy-start.3 = (f32[2048]{0:T(1024)S(1)}, f32[2048]{0:T(1024)}, u32[]{:S(2)}) copy-start(f32[2048]{0:T(1024)} %param.14) | copy-start | bytes 24580
  66.9 52.9 %copy-start.4 = (s32[32]{0:T(128)S(1)}, s32[32]{0:T(128)}, u32[]{:S(2)}) copy-start(s32[32]{0:T(128)} %param.11) | copy-start | bytes 388
  66.9 52.9 %copy-start.5 = (s32[32]{0:T(128)S(1)}, s32[32]{0:T(128)}, u32[]{:S(2)}) copy-start(s32[32]{0:T(128)} %param.12) | copy-start | bytes 388
  114.6 10.1 %all-to-all-start.1 = ((bf16[8,2,1024]{2,1,0:T(2,128)(2,1)}), bf16[8,2,1024]{2,1,0:T(2,128)(2,1)S(1)}, u32[]{:S(2)}, u32[]{:S(2)}) async-start(bf16[8,2,1024]{2,1,0:T(2,128)(2,1)} %reshape.288), calls=%async_computation.1 | async-start | bytes 65536 | tf_op jit(solution)/shard_map/all_to_all | solution.py:78
  124.6 19.6 %all-to-all-start = ((bf16[4,2,2048]{2,1,0:T(2,128)(2,1)}), bf16[4,2,2048]{2,1,0:T(2,128)(2,1)S(1)}, u32[]{:S(2)}, u32[]{:S(2)}) async-start(bf16[4,2,2048]{2,1,0:T(2,128)(2,1)} %reshape.290), calls=%async_computation | async-start | bytes 65536 | tf_op jit(solution)/shard_map/all_to_all | solution.py:93
where the time goes:
time: 178 us; the launch traced here: 177 us
  local copies, waits for them, and re-layouts  100 us (56%)
  matrix products  38.2 us (21%)
  blocking collectives  22.9 us (13%)
  starting transfers between devices  10.1 us (6%)
  waiting for transfers between devices  2.85 us (2%)
  other arithmetic  2.66 us (1%)
    gather x1, local copies, waits for them, and re-layouts, transform(): flat_imag = jnp.take(final_imag.reshape(count_pairs, -1), shifted, axis=1)  45.5 us
    gather x1, local copies, waits for them, and re-layouts, transform(): flat_real = jnp.take(final_real.reshape(count_pairs, -1), shifted, axis=1)  45.5 us
    dot_general x1, matrix products, shards(): lax.dot_general(row_panel, permuted, contract, preferred_element_type=jnp...  24.2 us
    all_gather x1, blocking collectives, shards(): column_panel = lax.all_gather(blocks, 'row', axis=0, tiled=True)  13.9 us
    all_gather x1, blocking collectives, shards(): row_panel = lax.all_gather(row_blocks, 'col', axis=0, tiled=True)  9.03 us
    all_to_all x1, starting transfers between devices, shards(): lax.all_to_all(coefficients, 'col', split_axis=1, concat_axis=0, tiled=True)  5.21 us
    all_to_all x1, starting transfers between devices, shards(): lax.all_to_all(coefficients, 'row', split_axis=1, concat_axis=0, tiled=True)  4.86 us
  transfers between devices with their start and end apart: 2, of which 1 were waited for; matrix products, arithmetic and copies ran while one was open for 2% of the time, Pallas kernels for 0%

commit v1 on v0

v1 whole, which is shorter than its diff:
```python
import functools
import math

import jax
import jax.numpy as jnp
import numpy as np
from jax import lax
from jax.experimental import pallas as pl
from jax.experimental.pallas import tpu as pltpu
from jax.sharding import PartitionSpec as P

MESH = pl.DeviceIdType.MESH
LANES = 128


def split(values):
    high = values.astype(jnp.bfloat16)
    low = (values - high.astype(jnp.float32)).astype(jnp.bfloat16)
    return high, low


def fourier_tables(points):
    counter = np.arange(points)
    angles = (counter[:, None] * counter[None, :] % points) * (2.0 * math.pi / points)
    cosine, sine = np.cos(angles), np.sin(angles)
    along_z = np.concatenate([cosine, -sine, -sine, -cosine], axis=1)
    along_y = np.block([[cosine, sine], [-sine, cosine]])
    upper = points // 2
    along_x = np.concatenate([cosine[:upper], sine[:upper]], axis=1) * float(points) ** (-1.5)
    tables = []
    for table in (along_z, along_y, along_x):
        single = table.astype(np.float32)
        high = single.astype(jnp.bfloat16)
        low = (single - high.astype(np.float32)).astype(jnp.bfloat16)
        tables += [high, low]
    return tables


def dot(left, right):
    return lax.dot_general(
        left, right, (((1,), (0,)), ((), ())), preferred_element_type=jnp.float32
    )


def transform_kernel(
    x_ref, index_ref, zh_ref, zl_ref, yh_ref, yl_ref, xh_ref, xl_ref,
    by_row_ref, by_col_ref,
    first, second, spectrum, picked,
):
    points = x_ref.shape[0]
    upper = points // 2
    wide = 2 * points
    step = 8

    zh, zl = zh_ref[...], zl_ref[...]

    @pl.loop(0, points // step)
    def _(block):
        start = pl.multiple_of(block * step, step)
        data = x_ref[pl.ds(start, step)].reshape(step * points, points)
        rows = pl.ds(pl.multiple_of(start * points, step * points), step * points)
        first[rows, :] = dot(data, zh) + dot(data, zl)

    yh, yl = yh_ref[...], yl_ref[...]

    @pl.loop(0, points // 2, unroll=2)
    def _(pair):
        blocks = []
        for side in range(2):
            rows = pl.ds(pl.multiple_of((2 * pair + side) * points, points), points)
            blocks.append(jnp.concatenate([first[rows, :wide], first[rows, wide:]], axis=0))
        high, low = split(jnp.concatenate(blocks, axis=1))
        result = dot(yh, high) + (dot(yh, low) + dot(yl, high))
        for side in range(2):
            rows = pl.ds(pl.multiple_of((2 * pair + side) * wide, wide), wide)
            second[rows, :] = result[:, side * wide:(side + 1) * wide]

    xh, xl = xh_ref[...], xl_ref[...]
    per_group = spectrum.shape[1] // LANES
    groups = points // 2 // per_group
    half_rows = groups * upper
    lane = lax.broadcasted_iota(jnp.int32, (upper, wide), 1)

    for group in range(groups):

        @pl.loop(0, per_group, unroll=2)
        def _(place):
            base = 2 * (group * per_group + place)
            blocks = []
            for side in range(2):
                straight = second[pl.ds(base + side, points, stride=wide), :]
                turned = second[pl.ds(base + side + points, points, stride=wide), :]
                blocks.append(jnp.concatenate([straight, turned], axis=0))
            high, low = split(jnp.concatenate(blocks, axis=1))
            result = dot(xh, high) + (dot(xh, low) + dot(xl, high))
            even, odd = result[:, :wide], result[:, wide:]
            real = jnp.where(lane < points, even, pltpu.roll(odd, points, 1))
            imag = -jnp.where(lane < points, pltpu.roll(even, points, 1), odd)
            columns = pl.ds(pl.multiple_of(place * LANES, LANES), LANES)
            spectrum[group * upper:(group + 1) * upper, columns] = real.astype(jnp.bfloat16)
            spectrum[half_rows + group * upper:half_rows + (group + 1) * upper, columns] = (
                imag.astype(jnp.bfloat16)
            )

    depth = spectrum.shape[1]
    count = index_ref.shape[1]
    width = 256
    part = 256
    local = lax.broadcasted_iota(jnp.int32, (part, width), 0).astype(jnp.float32).astype(jnp.bfloat16)
    row_of = lax.broadcasted_iota(jnp.int32, (half_rows, width), 0)
    one = jnp.ones((part, width), jnp.bfloat16)
    zero = jnp.zeros((part, width), jnp.bfloat16)

    @pl.loop(0, count // width)
    def _(chunk):
        start = pl.multiple_of(chunk * width, width)
        index = index_ref[:, pl.ds(start, width)]
        column = index % depth
        upper_part = index // depth
        row = (upper_part % groups) * upper + upper_part // groups
        total = jnp.zeros((2 * half_rows, width), jnp.float32)
        for at in range(depth // part):
            shifted = (column - at * part).astype(jnp.float32).astype(jnp.bfloat16)
            chosen = jnp.where(local == jnp.broadcast_to(shifted, local.shape), one, zero)
            total = total + dot(spectrum[:, at * part:(at + 1) * part], chosen)
        mask = row_of == row
        real = jnp.sum(jnp.where(mask, total[:half_rows], 0.0), axis=0, keepdims=True)
        imag = jnp.sum(jnp.where(mask, total[half_rows:], 0.0), axis=0, keepdims=True)
        for side in range(width // LANES):
            line = chunk * (width // LANES) + side
            lanes = slice(side * LANES, (side + 1) * LANES)
            picked[pl.ds(line, 1), :] = real[:, lanes]
            picked[pl.ds(count // LANES + line, 1), :] = imag[:, lanes]

    for ref in (by_row_ref, by_col_ref):
        height = ref.shape[1]
        for block in range(ref.shape[0]):
            ref[block] = picked[block * height:(block + 1) * height, :].astype(jnp.bfloat16)


def transform(product, pw_index, row_count, col_count):
    points = product.shape[0]
    count = pw_index.shape[0]
    lines = 2 * count // LANES
    tables = [jnp.asarray(table) for table in fourier_tables(points)]
    depth = 1024
    whole = pl.BlockSpec(memory_space=pltpu.VMEM)
    return pl.pallas_call(
        transform_kernel,
        out_shape=(
            jax.ShapeDtypeStruct((row_count, lines // row_count, LANES), jnp.bfloat16),
            jax.ShapeDtypeStruct((col_count, lines // col_count, LANES), jnp.bfloat16),
        ),
        in_specs=[whole] * (2 + len(tables)),
        out_specs=(whole, whole),
        scratch_shapes=[
            pltpu.VMEM((points * points, 4 * points), jnp.float32),
            pltpu.VMEM((points * 2 * points, 2 * points), jnp.float32),
            pltpu.VMEM((points**3 // depth, depth), jnp.bfloat16),
            pltpu.VMEM((lines, LANES), jnp.float32),
        ],
        name="spectrum",
    )(product, pw_index.reshape(1, count), *tables)


def exchange_kernel(
    by_row, by_col, row_panel, col_panel,
    row_send, row_recv, col_send, col_recv,
    share_send, share_recv, pass_send, pass_recv, own_sem,
):
    rows, cols = row_panel.shape[:2]
    r, c = lax.axis_index("row"), lax.axis_index("col")

    barrier = pltpu.get_barrier_semaphore()

    def each(count, action):
        def body(step, carry):
            action(step)
            return carry

        lax.fori_loop(1, count, body, 0)

    each(rows, lambda i: pl.semaphore_signal(
        barrier, inc=1, device_id=(lax.rem(r + i, rows), c), device_id_type=MESH))
    each(cols, lambda k: pl.semaphore_signal(
        barrier, inc=1, device_id=(r, lax.rem(c + k, cols)), device_id_type=MESH))
    pl.semaphore_wait(barrier, rows + cols - 2)

    def remote(source, target, send, recv, device):
        return pltpu.make_async_remote_copy(
            src_ref=source, dst_ref=target, send_sem=send, recv_sem=recv,
            device_id=device, device_id_type=MESH)

    def row_copy(i, source):
        return remote(
            by_row.at[lax.rem(r + i, rows)], row_panel.at[source, c],
            row_send.at[i], row_recv.at[i], (lax.rem(r + i, rows), c))

    def col_copy(k, source):
        return remote(
            by_col.at[lax.rem(c + k, cols)], col_panel.at[r, source],
            col_send.at[k], col_recv.at[k], (r, lax.rem(c + k, cols)))

    def share(i, k, held, source):
        return remote(
            held, row_panel.at[lax.rem(r - i + rows, rows), source],
            share_send.at[i, k], share_recv.at[i, k], (r, lax.rem(c + k, cols)))

    def hand_on(i, source):
        return remote(
            col_panel.at[r], col_panel.at[source],
            pass_send.at[i], pass_recv.at[i], (lax.rem(r + i, rows), c))

    each(rows, lambda i: row_copy(i, r).start())
    each(cols, lambda k: col_copy(k, c).start())
    own_row = pltpu.make_async_copy(by_row.at[r], row_panel.at[r, c], own_sem.at[0])
    own_col = pltpu.make_async_copy(by_col.at[c], col_panel.at[r, c], own_sem.at[1])
    own_row.start()
    own_col.start()
    each(cols, lambda k: share(0, k, by_row.at[r], c).start())
    own_row.wait()
    own_col.wait()
    each(cols, lambda k: col_copy(k, lax.rem(c - k + cols, cols)).wait_recv())
    each(rows, lambda i: hand_on(i, r).start())

    def forward(i):
        source = lax.rem(r - i + rows, rows)
        row_copy(i, source).wait_recv()
        each(cols, lambda k: share(i, k, row_panel.at[source, c], c).start())

    each(rows, forward)

    def finish(i, carry):
        held = row_panel.at[lax.rem(r - i + rows, rows), c]

        def ending(k):
            share(i, k, held, lax.rem(c - k + cols, cols)).wait_recv()
            share(i, k, held, c).wait_send()

        each(cols, ending)
        return carry

    each(rows, lambda i: row_copy(i, r).wait_send())
    each(cols, lambda k: col_copy(k, c).wait_send())

    def passed(i):
        hand_on(i, lax.rem(r - i + rows, rows)).wait_recv()
        hand_on(i, r).wait_send()

    each(rows, passed)
    lax.fori_loop(0, rows, finish, 0)


def exchange(by_row, by_col):
    rows, cols = by_row.shape[0], by_col.shape[0]
    whole = pl.BlockSpec(memory_space=pltpu.VMEM)
    dma = pltpu.SemaphoreType.DMA
    return pl.pallas_call(
        exchange_kernel,
        out_shape=(
            jax.ShapeDtypeStruct((rows, cols) + by_row.shape[1:], jnp.bfloat16),
            jax.ShapeDtypeStruct((rows, cols) + by_col.shape[1:], jnp.bfloat16),
        ),
        in_specs=[whole, whole],
        out_specs=(whole, whole),
        scratch_shapes=[
            dma((rows,)), dma((rows,)), dma((cols,)), dma((cols,)),
            dma((rows, cols)), dma((rows, cols)), dma((rows,)), dma((rows,)), dma((2,)),
        ],
        compiler_params=pltpu.CompilerParams(collective_id=0, has_side_effects=True),
        name="exchange",
    )(by_row, by_col)


def product_kernel(row_ref, col_ref, weight_ref, out_ref, row_lines, col_lines, left, right):
    pairs = row_ref.shape[0]

    @pl.when(pl.program_id(0) == 0)
    def _():
        for ref, lines, is_left in ((row_ref, row_lines, True), (col_ref, col_lines, False)):
            if len(ref.shape) == 3:
                height = ref.shape[1]
                lines[...] = ref[...].astype(jnp.float32).reshape(lines.shape)
            else:
                height = ref.shape[1] // LANES
            for block in range(height):
                lanes = slice(block * LANES, (block + 1) * LANES)
                if len(ref.shape) == 3:
                    values = lines[pl.ds(block, pairs, stride=height), :]
                else:
                    values = ref[:, lanes].astype(jnp.float32)
                if is_left:
                    left[lanes, :] = values.T.astype(jnp.bfloat16)
                else:
                    for freq in range(out_ref.shape[0]):
                        right[freq, :, lanes] = (
                            values * weight_ref[:, freq:freq + 1]
                        ).astype(jnp.bfloat16)

    height = out_ref.shape[1]
    rows = pl.ds(pl.multiple_of(pl.program_id(0) * height, height), height)
    panel = left[rows, :]
    for freq in range(out_ref.shape[0]):
        out_ref[freq] = dot(panel, right[freq])


def product(row_panel, col_panel, weights):
    pairs, freq_count = weights.shape
    row_width = row_panel.shape[2] * LANES
    col_width = col_panel.shape[2] * LANES
    panels = []
    lines = []
    for panel in (row_panel, col_panel):
        height = panel.shape[2]
        if height % 16 == 0:
            panels.append(panel.reshape(pairs, height, LANES))
            lines.append(pltpu.VMEM((pairs * height, LANES), jnp.float32))
        else:
            panels.append(panel.reshape(pairs, height * LANES))
            lines.append(pltpu.VMEM((8, LANES), jnp.float32))
    block = min(256, row_width)
    whole = pl.BlockSpec(memory_space=pltpu.VMEM)
    return pl.pallas_call(
        product_kernel,
        grid=(row_width // block,),
        out_shape=jax.ShapeDtypeStruct((freq_count, row_width, col_width), jnp.float32),
        in_specs=[whole, whole, whole],
        out_specs=pl.BlockSpec((freq_count, block, col_width), lambda i: (0, i, 0)),
        scratch_shapes=lines + [
            pltpu.VMEM((row_width, pairs), jnp.bfloat16),
            pltpu.VMEM((freq_count, pairs, col_width), jnp.bfloat16),
        ],
        name="product",
    )(*panels, weights)


def lookup(indices, table):
    slots = jnp.arange(table.shape[0], dtype=jnp.int32)
    return jnp.sum(jnp.where(indices[:, None] == slots[None, :], table[None, :], 0.0), axis=1)


def pair_weights(valence_band, conduction_band, valence_energy, conduction_energy, imag_freq):
    gap = lookup(conduction_band, conduction_energy) - lookup(valence_band, valence_energy)
    total = valence_band.shape[0]
    return (
        -4.0
        * gap[:, None]
        / (gap[:, None] ** 2 + imag_freq[None, :] ** 2)
        / jnp.sqrt(jnp.float32(total))
    )


def shards(
    pair_products,
    pw_index,
    valence_band,
    conduction_band,
    valence_energy,
    conduction_energy,
    imag_freq,
):
    rows, cols = lax.axis_size("row"), lax.axis_size("col")
    by_row, by_col = transform(pair_products[0], pw_index, rows, cols)
    row_panel, col_panel = exchange(by_row, by_col)
    weights = pair_weights(
        valence_band, conduction_band, valence_energy, conduction_energy, imag_freq
    )
    return product(row_panel, col_panel, weights)


def solution(mesh):
    in_specs = (P(("row", "col"), None, None, None), P(), P(), P(), P(), P(), P())
    out_specs = P(None, "row", "col")
    return jax.shard_map(shards, mesh=mesh, in_specs=in_specs, out_specs=out_specs, check_vma=False)
```

time: 178 us -> 68.1 us (0.38)
  local copies, waits for them, and re-layouts: 100 us -> 0 us
  Pallas kernels: 0 us -> 65.4 us
  matrix products: 38.2 us -> 0 us
  blocking collectives: 22.9 us -> 0 us
  starting transfers between devices: 10.1 us -> 0 us
  waiting for transfers between devices: 2.85 us -> 0 us
    gather x2 -> x0, local copies, waits for them, and re-layouts: 91.1 us -> none  [the longest x1 45.5 us: transform(): flat_imag = jnp.take(final_imag.reshape(count_pairs, -1), shifted, axis=1)]
    pallas_call x0 -> x3, Pallas kernels: none -> 65.4 us  [the longest x1 25 us: transform(): pl.pallas_call(transform_kernel, out_shape=(jax.ShapeDtypeStruct((row_cou...]
    dot_general x10 -> x0, matrix products: 38.2 us -> none  [the longest x1 24.2 us: shards(): lax.dot_general(row_panel, permuted, contract, preferred_element_type=jnp...]
    all_gather x2 -> x0, blocking collectives: 22.9 us -> none  [the longest x1 13.9 us: shards(): column_panel = lax.all_gather(blocks, 'row', axis=0, tiled=True)]
    all_to_all x2 -> x0, starting transfers between devices: 10.1 us -> none  [the longest x1 5.21 us: shards(): lax.all_to_all(coefficients, 'col', split_axis=1, concat_axis=0, tiled=True)]
    all_to_all x2 -> x0, waiting for transfers between devices: 2.85 us -> none  [the longest x1 2.85 us: shards(): lax.all_to_all(coefficients, 'col', split_axis=1, concat_axis=0, tiled=True)]
    unnamed x19 -> x0, local copies, waits for them, and re-layouts: 2.85 us -> none
    another operation x2 -> x0, local copies, waits for them, and re-layouts: 2.82 us -> none  [the longest x1 1.41 us: transform(): flat_real = jnp.take(final_real.reshape(count_pairs, -1), shifted, axis=1)]
  transfers between devices with their start and end apart: 2 -> 0, of which waited for: 1 -> 0; matrix products, arithmetic and copies ran while one was open for 2% -> 0% of each run, Pallas kernels for 0% -> 0%
where the time goes in v1:
time: 68.1 us; the launch traced here: 67.8 us
  Pallas kernels  65.4 us (96%)
  other arithmetic  2.41 us (4%)
    pallas_call x1, Pallas kernels, transform(): pl.pallas_call(transform_kernel, out_shape=(jax.ShapeDtypeStruct((row_cou...  25 us
    pallas_call x1, Pallas kernels, product(): pl.pallas_call(product_kernel, grid=(row_width // block,), out_shape=jax....  24.7 us
    pallas_call x1, Pallas kernels, exchange(): pl.pallas_call(exchange_kernel, out_shape=(jax.ShapeDtypeStruct((rows, co...  15.6 us

profile of v1, /device:TPU:0, one launch (start us, length us, event | category | flops | bytes accessed | tf_op | source)
XLA Modules:
  0.0 67.8 jit_solution(8338264566804876908)
XLA Ops:
  0.0 0.7 %integer_pow.13 = f32[2]{0:T(128)S(1)} multiply(f32[2]{0:T(128)} %param.19, f32[2]{0:T(128)} %param.19) | non-fusion elementwise | flops 2 | bytes 24 | tf_op jit(solution)/shard_map/integer_pow | solution.py:348
  0.7 1.0 %select_reduce_fusion = (f32[32]{0:T(128)S(1)}, f32[32]{0:T(128)S(1)}) fusion(f32[2048]{0:T(1024)} %param.17, s32[32]{0:T(128)} %param.15, f32[2048]{0:T(1024)} %param.18, s32[32]{0:T(128)} %param.16), kind=kLoop, calls=%fused_computation | loop fusion | flops 393152 | bytes 16896 | tf_op jit(solution)/shard_map/reduce_sum | solution.py:339
  1.7 0.7 %divide_multiply_fusion.weight_ref = f32[32,2]{1,0:T(8,128)} fusion(f32[32]{0:T(128)S(1)} %get-tuple-element.14, f32[2]{0:T(128)S(1)} %integer_pow.13, f32[32]{0:T(128)S(1)} %get-tuple-element.13), kind=kLoop, calls=%fused_computation.4 | loop fusion | flops 192 | bytes 520 | tf_op jit(solution)/shard_map/div | solution.py:346
  2.4 25.0 %spectrum.1 = (bf16[4,32,128]{2,1,0:T(8,128)(2,1)}, bf16[8,16,128]{2,1,0:T(8,128)(2,1)}) custom-call(bf16[64,64,64]{2,1,0:T(8,128)(2,1)} %bitcast.4, s32[1,8192]{1,0:T(1,128)} %bitcast.7, bf16[64,256]{1,0:T(8,128)(2,1)} %constant.19.clone.zh_ref, bf16[64,256]{1,0:T(8,128)(2,1)} %constant.20.clone.zl_ref, bf16[128,128]{1,0:T(8,128)(2,1)} %constant.21.clone.yh_ref, ...), custom_call_target="tpu_custom_call" | custom-call | tf_op jit(solution)/shard_map/spectrum/pallas_call | solution.py:148
  27.5 15.6 %exchange.1 = (bf16[4,8,32,128]{3,2,1,0:T(8,128)(2,1)}, bf16[4,8,16,128]{3,2,1,0:T(8,128)(2,1)}) custom-call(bf16[4,32,128]{2,1,0:T(8,128)(2,1)} %get-tuple-element.9.by_row, bf16[8,16,128]{2,1,0:T(8,128)(2,1)} %get-tuple-element.10.by_col), custom_call_target="tpu_custom_call" | custom-call | tf_op jit(solution)/shard_map/exchange/pallas_call | solution.py:258
  43.1 24.7 %product.1 = f32[2,4096,2048]{2,1,0:T(8,128)} custom-call(bf16[32,32,128]{2,1,0:T(8,128)(2,1)} %bitcast.5, bf16[32,16,128]{2,1,0:T(8,128)(2,1)} %bitcast.6, f32[32,2]{1,0:T(8,128)} %divide_multiply_fusion.weight_ref), custom_call_target="tpu_custom_call" | custom-call | tf_op jit(solution)/shard_map/product/pallas_call | solution.py:323
  (1 shorter events, 0.0 us)

commit v2 on v1

--- a/solution.py
+++ b/solution.py
@@ -23,17 +23,20 @@
     counter = np.arange(points)
     angles = (counter[:, None] * counter[None, :] % points) * (2.0 * math.pi / points)
     cosine, sine = np.cos(angles), np.sin(angles)
-    along_z = np.concatenate([cosine, -sine, -sine, -cosine], axis=1)
-    along_y = np.block([[cosine, sine], [-sine, cosine]])
     upper = points // 2
-    along_x = np.concatenate([cosine[:upper], sine[:upper]], axis=1) * float(points) ** (-1.5)
-    tables = []
-    for table in (along_z, along_y, along_x):
+
+    def halves(table):
         single = table.astype(np.float32)
         high = single.astype(jnp.bfloat16)
-        low = (single - high.astype(np.float32)).astype(jnp.bfloat16)
-        tables += [high, low]
-    return tables
+        return high, (single - high.astype(np.float32)).astype(jnp.bfloat16)
+
+    along_z = np.concatenate(halves(np.concatenate([cosine, -sine], axis=1)), axis=0)
+    high, low = halves(np.concatenate([cosine, sine], axis=0))
+    along_y = np.concatenate([high, high, low], axis=1)
+    scale = float(points) ** (-1.5)
+    high, low = halves(np.concatenate([cosine[:upper], sine[:upper]], axis=0) * scale)
+    along_x = np.concatenate([high, high, low], axis=1)
+    return [along_z, along_y, along_x]
 
 
 def dot(left, right):
@@ -43,59 +46,59 @@
 
 
 def transform_kernel(
-    x_ref, index_ref, zh_ref, zl_ref, yh_ref, yl_ref, xh_ref, xl_ref,
+    x_ref, index_ref, z_ref, y_ref, x_table_ref,
     by_row_ref, by_col_ref,
-    first, second, spectrum, picked,
+    planes, spectrum, picked,
 ):
     points = x_ref.shape[0]
     upper = points // 2
     wide = 2 * points
     step = 8
-
-    zh, zl = zh_ref[...], zl_ref[...]
-
-    @pl.loop(0, points // step)
+    along_z, along_y, along_x = z_ref[...], y_ref[...], x_table_ref[...]
+    sign = jnp.where(lax.broadcasted_iota(jnp.int32, (points, wide), 1) < points, 1.0, -1.0)
+
+    @pl.loop(0, points // step, unroll=2)
     def _(block):
         start = pl.multiple_of(block * step, step)
         data = x_ref[pl.ds(start, step)].reshape(step * points, points)
-        rows = pl.ds(pl.multiple_of(start * points, step * points), step * points)
-        first[rows, :] = dot(data, zh) + dot(data, zl)
-
-    yh, yl = yh_ref[...], yl_ref[...]
-
-    @pl.loop(0, points // 2, unroll=2)
-    def _(pair):
-        blocks = []
-        for side in range(2):
-            rows = pl.ds(pl.multiple_of((2 * pair + side) * points, points), points)
-            blocks.append(jnp.concatenate([first[rows, :wide], first[rows, wide:]], axis=0))
-        high, low = split(jnp.concatenate(blocks, axis=1))
-        result = dot(yh, high) + (dot(yh, low) + dot(yl, high))
-        for side in range(2):
-            rows = pl.ds(pl.multiple_of((2 * pair + side) * wide, wide), wide)
-            second[rows, :] = result[:, side * wide:(side + 1) * wide]
-
-    xh, xl = xh_ref[...], xl_ref[...]
+        lines = dot(jnp.concatenate([data, data], axis=1), along_z)
+        high, low = split(lines)
+        for pair in range(step // 2):
+            blocks = []
+            for side in range(2):
+                rows = slice((2 * pair + side) * points, (2 * pair + side + 1) * points)
+                blocks.append(jnp.concatenate([high[rows], low[rows], high[rows]], axis=0))
+            result = dot(along_y, jnp.concatenate(blocks, axis=1))
+            for side in range(2):
+                part = result[:, side * wide:(side + 1) * wide]
+                rows = pl.ds(pl.multiple_of((start + 2 * pair + side) * points, points), points)
+                planes[rows, :] = part[:points] + sign * pltpu.roll(part[points:], points, 1)
+
     per_group = spectrum.shape[1] // LANES
     groups = points // 2 // per_group
     half_rows = groups * upper
-    lane = lax.broadcasted_iota(jnp.int32, (upper, wide), 1)
+    first_half = lax.broadcasted_iota(jnp.int32, (upper, wide), 1) < points
 
     for group in range(groups):
 
-        @pl.loop(0, per_group, unroll=2)
+        @pl.loop(0, per_group, unroll=8)
         def _(place):
             base = 2 * (group * per_group + place)
             blocks = []
             for side in range(2):
-                straight = second[pl.ds(base + side, points, stride=wide), :]
-                turned = second[pl.ds(base + side + points, points, stride=wide), :]
-                blocks.append(jnp.concatenate([straight, turned], axis=0))
-            high, low = split(jnp.concatenate(blocks, axis=1))
-            result = dot(xh, high) + (dot(xh, low) + dot(xl, high))
-            even, odd = result[:, :wide], result[:, wide:]
-            real = jnp.where(lane < points, even, pltpu.roll(odd, points, 1))
-            imag = -jnp.where(lane < points, pltpu.roll(even, points, 1), odd)
+                high, low = split(planes[pl.ds(base + side, points, stride=points), :])
+                blocks.append(jnp.concatenate([high, low, high], axis=0))
+            result = dot(along_x, jnp.concatenate(blocks, axis=1))
+            even_cos, odd_cos = result[:upper, :wide], result[:upper, wide:]
+            even_sin, odd_sin = result[upper:, :wide], result[upper:, wide:]
+
+            def join(left, right, turn_left, turn_right):
+                left = pltpu.roll(left, points, 1) if turn_left else left
+                right = pltpu.roll(right, points, 1) if turn_right else right
+                return jnp.where(first_half, left, right)
+
+            real = join(even_cos, odd_cos, False, True) + join(even_sin, odd_sin, True, False)
+            imag = join(even_sin, odd_sin, False, True) - join(even_cos, odd_cos, True, False)
             columns = pl.ds(pl.multiple_of(place * LANES, LANES), LANES)
             spectrum[group * upper:(group + 1) * upper, columns] = real.astype(jnp.bfloat16)
             spectrum[half_rows + group * upper:half_rows + (group + 1) * upper, columns] = (
@@ -111,7 +114,7 @@
     one = jnp.ones((part, width), jnp.bfloat16)
     zero = jnp.zeros((part, width), jnp.bfloat16)
 
-    @pl.loop(0, count // width)
+    @pl.loop(0, count // width, unroll=8)
     def _(chunk):
         start = pl.multiple_of(chunk * width, width)
         index = index_ref[:, pl.ds(start, width)]
@@ -154,8 +157,7 @@
         in_specs=[whole] * (2 + len(tables)),
         out_specs=(whole, whole),
         scratch_shapes=[
-            pltpu.VMEM((points * points, 4 * points), jnp.float32),
-            pltpu.VMEM((points * 2 * points, 2 * points), jnp.float32),
+            pltpu.VMEM((points * points, 2 * points), jnp.float32),
             pltpu.VMEM((points**3 // depth, depth), jnp.bfloat16),
             pltpu.VMEM((lines, LANES), jnp.float32),
         ],
@@ -163,8 +165,24 @@
     )(product, pw_index.reshape(1, count), *tables)
 
 
+def column_of(row):
+    size = row.shape[1]
+    here = lax.broadcasted_iota(jnp.int32, (size, size), 0)
+    there = lax.broadcasted_iota(jnp.int32, (size, size), 1)
+    return jnp.sum(jnp.where(here == there, row, 0.0), axis=1, keepdims=True)
+
+
+def lookup(indices, table):
+    column = column_of(indices.astype(jnp.float32))
+    slots = lax.broadcasted_iota(jnp.int32, (column.shape[0], table.shape[1]), 1)
+    return jnp.sum(
+        jnp.where(column == slots.astype(jnp.float32), table, 0.0), axis=1, keepdims=True
+    )
+
+
 def exchange_kernel(
-    by_row, by_col, row_panel, col_panel,
+    by_row, by_col, valence_band, conduction_band, valence_energy, conduction_energy, imag_freq,
+    row_panel, col_panel, weights,
     row_send, row_recv, col_send, col_recv,
     share_send, share_recv, pass_send, pass_recv, own_sem,
 ):
@@ -218,6 +236,13 @@
     own_row.start()
     own_col.start()
     each(cols, lambda k: share(0, k, by_row.at[r], c).start())
+    gap = lookup(conduction_band[...], conduction_energy[...]) - lookup(
+        valence_band[...], valence_energy[...]
+    )
+    root = math.sqrt(gap.shape[0])
+    for freq in range(weights.shape[1]):
+        omega = imag_freq[:, freq:freq + 1]
+        weights[:, freq:freq + 1] = -4.0 * gap / (gap * gap + omega * omega) / root
     own_row.wait()
     own_col.wait()
     each(cols, lambda k: col_copy(k, lax.rem(c - k + cols, cols)).wait_recv())
@@ -251,7 +276,8 @@
     lax.fori_loop(0, rows, finish, 0)
 
 
-def exchange(by_row, by_col):
+def exchange(by_row, by_col, *bands):
+    bands = [values.reshape(1, -1) for values in bands]
     rows, cols = by_row.shape[0], by_col.shape[0]
     whole = pl.BlockSpec(memory_space=pltpu.VMEM)
     dma = pltpu.SemaphoreType.DMA
@@ -260,48 +286,66 @@
         out_shape=(
             jax.ShapeDtypeStruct((rows, cols) + by_row.shape[1:], jnp.bfloat16),
             jax.ShapeDtypeStruct((rows, cols) + by_col.shape[1:], jnp.bfloat16),
+            jax.ShapeDtypeStruct((bands[0].shape[1], bands[-1].shape[1]), jnp.float32),
         ),
-        in_specs=[whole, whole],
-        out_specs=(whole, whole),
+        in_specs=[whole] * (2 + len(bands)),
+        out_specs=(whole, whole, whole),
         scratch_shapes=[
             dma((rows,)), dma((rows,)), dma((cols,)), dma((cols,)),
             dma((rows, cols)), dma((rows, cols)), dma((rows,)), dma((rows,)), dma((2,)),
         ],
         compiler_params=pltpu.CompilerParams(collective_id=0, has_side_effects=True),
         name="exchange",
-    )(by_row, by_col)
-
-
-def product_kernel(row_ref, col_ref, weight_ref, out_ref, row_lines, col_lines, left, right):
+    )(by_row, by_col, *bands)
+
+
+def product_kernel(row_ref, col_ref, weight_ref, out_ref, row_lines, col_lines, left, right, ring, sems):
     pairs = row_ref.shape[0]
-
-    @pl.when(pl.program_id(0) == 0)
-    def _():
-        for ref, lines, is_left in ((row_ref, row_lines, True), (col_ref, col_lines, False)):
+    freq_count, row_width, _ = out_ref.shape
+    slots, height = ring.shape[0], ring.shape[1]
+
+    for ref, lines, is_left in ((row_ref, row_lines, True), (col_ref, col_lines, False)):
+        if len(ref.shape) == 3:
+            blocks = ref.shape[1]
+            lines[...] = ref[...].astype(jnp.float32).reshape(lines.shape)
+        else:
+            blocks = ref.shape[1] // LANES
+        for block in range(blocks):
+            lanes = slice(block * LANES, (block + 1) * LANES)
             if len(ref.shape) == 3:
-                height = ref.shape[1]
-                lines[...] = ref[...].astype(jnp.float32).reshape(lines.shape)
+                values = lines[pl.ds(block, pairs, stride=blocks), :]
             else:
-                height = ref.shape[1] // LANES
-            for block in range(height):
-                lanes = slice(block * LANES, (block + 1) * LANES)
-                if len(ref.shape) == 3:
-                    values = lines[pl.ds(block, pairs, stride=height), :]
-                else:
-                    values = ref[:, lanes].astype(jnp.float32)
-                if is_left:
-                    left[lanes, :] = values.T.astype(jnp.bfloat16)
-                else:
-                    for freq in range(out_ref.shape[0]):
-                        right[freq, :, lanes] = (
-                            values * weight_ref[:, freq:freq + 1]
-                        ).astype(jnp.bfloat16)
-
-    height = out_ref.shape[1]
-    rows = pl.ds(pl.multiple_of(pl.program_id(0) * height, height), height)
-    panel = left[rows, :]
-    for freq in range(out_ref.shape[0]):
-        out_ref[freq] = dot(panel, right[freq])
+                values = ref[:, lanes].astype(jnp.float32)
+            if is_left:
+                left[lanes, :] = values.T.astype(jnp.bfloat16)
+            else:
+                for freq in range(freq_count):
+                    right[freq, :, lanes] = (
+                        values * weight_ref[:, freq:freq + 1]
+                    ).astype(jnp.bfloat16)
+
+    steps = row_width // height
+
+    def write(slot, freq, step):
+        rows = pl.ds(pl.multiple_of(step * height, height), height)
+        return pltpu.make_async_copy(ring.at[slot], out_ref.at[freq, rows], sems.at[slot])
+
+    @pl.loop(0, steps)
+    def _(step):
+        panel = left[pl.ds(pl.multiple_of(step * height, height), height), :]
+        for freq in range(freq_count):
+            unit = step * freq_count + freq
+            slot = lax.rem(unit, slots)
+
+            @pl.when(unit >= slots)
+            def _():
+                write(slot, freq, step).wait()
+
+            ring[slot] = dot(panel, right[freq])
+            write(slot, freq, step).start()
+
+    for slot in range(min(slots, steps * freq_count)):
+        write(slot, 0, 0).wait()
 
 
 def product(row_panel, col_panel, weights):
@@ -319,35 +363,21 @@
             panels.append(panel.reshape(pairs, height * LANES))
             lines.append(pltpu.VMEM((8, LANES), jnp.float32))
     block = min(256, row_width)
+    slots = 4
     whole = pl.BlockSpec(memory_space=pltpu.VMEM)
     return pl.pallas_call(
         product_kernel,
-        grid=(row_width // block,),
         out_shape=jax.ShapeDtypeStruct((freq_count, row_width, col_width), jnp.float32),
         in_specs=[whole, whole, whole],
-        out_specs=pl.BlockSpec((freq_count, block, col_width), lambda i: (0, i, 0)),
+        out_specs=pl.BlockSpec(memory_space=pl.ANY),
         scratch_shapes=lines + [
             pltpu.VMEM((row_width, pairs), jnp.bfloat16),
             pltpu.VMEM((freq_count, pairs, col_width), jnp.bfloat16),
+            pltpu.VMEM((slots, block, col_width), jnp.float32),
+            pltpu.SemaphoreType.DMA((slots,)),
         ],
         name="product",
     )(*panels, weights)
-
-
-def lookup(indices, table):
-    slots = jnp.arange(table.shape[0], dtype=jnp.int32)
-    return jnp.sum(jnp.where(indices[:, None] == slots[None, :], table[None, :], 0.0), axis=1)
-
-
-def pair_weights(valence_band, conduction_band, valence_energy, conduction_energy, imag_freq):
-    gap = lookup(conduction_band, conduction_energy) - lookup(valence_band, valence_energy)
-    total = valence_band.shape[0]
-    return (
-        -4.0
-        * gap[:, None]
-        / (gap[:, None] ** 2 + imag_freq[None, :] ** 2)
-        / jnp.sqrt(jnp.float32(total))
-    )
 
 
 def shards(
@@ -361,9 +391,9 @@
 ):
     rows, cols = lax.axis_size("row"), lax.axis_size("col")
     by_row, by_col = transform(pair_products[0], pw_index, rows, cols)
-    row_panel, col_panel = exchange(by_row, by_col)
-    weights = pair_weights(
-        valence_band, conduction_band, valence_energy, conduction_energy, imag_freq
+    row_panel, col_panel, weights = exchange(
+        by_row, by_col,
+        valence_band, conduction_band, valence_energy, conduction_energy, imag_freq,
     )
     return product(row_panel, col_panel, weights)
 

time: 68.1 us -> 51.3 us (0.75)
  Pallas kernels: 65.4 us -> 51 us
  other arithmetic: 2.41 us -> 0 us
    pallas_call x1, Pallas kernels: 25 us -> 12.2 us  [transform(): pl.pallas_call(transform_kernel, out_shape=(jax.ShapeDtypeStruct((row_cou...]
    pallas_call x1, Pallas kernels: 24.7 us -> 23.2 us  [product(): pl.pallas_call(product_kernel, out_shape=jax.ShapeDtypeStruct((freq_count...]
    reduce_sum x1 -> x0, other arithmetic: 0.98 us -> none  [lookup(): jnp.sum(jnp.where(indices[:, None] == slots[None, :], table[None, :], 0.0...]
    integer_pow x2 -> x0, other arithmetic: 0.74 us -> none  [the longest x1 0.73 us: pair_weights(): imag_freq[None, :] ** 2]
    div x1 -> x0, other arithmetic: 0.69 us -> none  [pair_weights(): -4.0 * gap[:, None] / (gap[:, None] ** 2 + imag_freq[None, :] ** 2)]
where the time goes in v2:
time: 51.3 us; the launch traced here: 51.1 us
  Pallas kernels  51 us (99%)
    pallas_call x1, Pallas kernels, product(): pl.pallas_call(product_kernel, out_shape=jax.ShapeDtypeStruct((freq_count...  23.2 us
    pallas_call x1, Pallas kernels, exchange(): pl.pallas_call(exchange_kernel, out_shape=(jax.ShapeDtypeStruct((rows, co...  15.6 us
    pallas_call x1, Pallas kernels, transform(): pl.pallas_call(transform_kernel, out_shape=(jax.ShapeDtypeStruct((row_cou...  12.2 us

profile of v2, /device:TPU:0, one launch (start us, length us, event | category | flops | bytes accessed | tf_op | source)
XLA Modules:
  0.0 51.1 jit_solution(8662319471091443674)
XLA Ops:
  0.0 12.2 %spectrum.1 = (bf16[4,32,128]{2,1,0:T(8,128)(2,1)}, bf16[8,16,128]{2,1,0:T(8,128)(2,1)}) custom-call(bf16[64,64,64]{2,1,0:T(8,128)(2,1)} %bitcast.9, s32[1,8192]{1,0:T(1,128)} %bitcast.12, bf16[128,128]{1,0:T(8,128)(2,1)} %constant.6.clone.z_ref, bf16[128,192]{1,0:T(8,128)(2,1)} %constant.7.clone.y_ref, bf16[64,192]{1,0:T(8,128)(2,1)} %constant.8.clone.x_table_ref), custom_call_target="tpu_custom_call" | custom-call | tf_op jit(solution)/shard_map/spectrum/pallas_call | solution.py:151
  12.2 15.6 %exchange.1 = (bf16[4,8,32,128]{3,2,1,0:T(8,128)(2,1)}, bf16[4,8,16,128]{3,2,1,0:T(8,128)(2,1)}, f32[32,2]{1,0:T(8,128)}) custom-call(bf16[4,32,128]{2,1,0:T(8,128)(2,1)} %get-tuple-element.10.by_row, bf16[8,16,128]{2,1,0:T(8,128)(2,1)} %get-tuple-element.11.by_col, s32[1,32]{1,0:T(1,128)} %bitcast.15, s32[1,32]{1,0:T(1,128)} %bitcast.16, ...), custom_call_target="tpu_custom_call" | custom-call | tf_op jit(solution)/shard_map/exchange/pallas_call | solution.py:284
  27.9 23.2 %product.1 = f32[2,4096,2048]{2,1,0:T(8,128)} custom-call(bf16[32,32,128]{2,1,0:T(8,128)(2,1)} %bitcast.10, bf16[32,16,128]{2,1,0:T(8,128)(2,1)} %bitcast.11, f32[32,2]{1,0:T(8,128)} %get-tuple-element.14.weight_ref), custom_call_target="tpu_custom_call" | custom-call | tf_op jit(solution)/shard_map/product/pallas_call | solution.py:368

commit v3 on v2

--- a/solution.py
+++ b/solution.py
@@ -1,4 +1,3 @@
-import functools
 import math
 
 import jax
@@ -45,11 +44,88 @@
     )
 
 
+def column_of(row):
+    size = row.shape[1]
+    here = lax.broadcasted_iota(jnp.int32, (size, size), 0)
+    there = lax.broadcasted_iota(jnp.int32, (size, size), 1)
+    return jnp.sum(jnp.where(here == there, row, 0.0), axis=1, keepdims=True)
+
+
+def lookup(indices, table):
+    column = column_of(indices.astype(jnp.float32))
+    slots = lax.broadcasted_iota(jnp.int32, (column.shape[0], table.shape[1]), 1)
+    return jnp.sum(
+        jnp.where(column == slots.astype(jnp.float32), table, 0.0), axis=1, keepdims=True
+    )
+
+
 def transform_kernel(
     x_ref, index_ref, z_ref, y_ref, x_table_ref,
-    by_row_ref, by_col_ref,
-    planes, spectrum, picked,
+    valence_band, conduction_band, valence_energy, conduction_energy, imag_freq,
+    row_panel, col_panel, weights,
+    planes, spectrum, picked, by_row, by_col,
+    row_send, row_recv, col_send, col_recv,
+    share_send, share_recv, pass_send, pass_recv,
 ):
+    rows, cols, tall = row_panel.shape[:3]
+    short = col_panel.shape[2]
+    phases = row_send.shape[0]
+    chunk_lines = tall // phases
+    r, c = lax.axis_index("row"), lax.axis_index("col")
+
+    def each(count, action):
+        def body(step, carry):
+            action(step)
+            return carry
+
+        lax.fori_loop(1, count, body, 0)
+
+    def ahead(i):
+        return lax.rem(r + i, rows)
+
+    def behind(i):
+        return lax.rem(r - i + rows, rows)
+
+    def onward(k):
+        return lax.rem(c + k, cols)
+
+    def back(k):
+        return lax.rem(c - k + cols, cols)
+
+    def remote(source, target, send, recv, device):
+        return pltpu.make_async_remote_copy(
+            src_ref=source, dst_ref=target, send_sem=send, recv_sem=recv,
+            device_id=device, device_id_type=MESH)
+
+    def lines_of(phase):
+        return pl.ds(phase * chunk_lines, chunk_lines)
+
+    def row_copy(phase, i, source):
+        return remote(
+            by_row.at[ahead(i), lines_of(phase)], row_panel.at[source, c, lines_of(phase)],
+            row_send.at[phase, i], row_recv.at[phase, i], (ahead(i), c))
+
+    def col_copy(k, source):
+        return remote(
+            by_col.at[onward(k)], col_panel.at[r, source],
+            col_send.at[k], col_recv.at[k], (r, onward(k)))
+
+    def share(phase, i, k, held, source):
+        return remote(
+            held, row_panel.at[behind(i), source, lines_of(phase)],
+            share_send.at[phase, i, k], share_recv.at[phase, i, k], (r, onward(k)))
+
+    def hand_on(i, source):
+        return remote(
+            col_panel.at[r], col_panel.at[source],
+            pass_send.at[i], pass_recv.at[i], (ahead(i), c))
+
+    barrier = pltpu.get_barrier_semaphore()
+    each(rows, lambda i: pl.semaphore_signal(
+        barrier, inc=1, device_id=(ahead(i), c), device_id_type=MESH))
+    each(cols, lambda k: pl.semaphore_signal(
+        barrier, inc=1, device_id=(r, onward(k)), device_id_type=MESH))
+
     points = x_ref.shape[0]
     upper = points // 2
     wide = 2 * points
@@ -114,9 +190,13 @@
     one = jnp.ones((part, width), jnp.bfloat16)
     zero = jnp.zeros((part, width), jnp.bfloat16)
 
-    @pl.loop(0, count // width, unroll=8)
-    def _(chunk):
-        start = pl.multiple_of(chunk * width, width)
+    lines_per_step = width // LANES
+    steps_per_block = chunk_lines // lines_per_step
+
+    def select(phase, step):
+        line = (step // steps_per_block) * tall + phase * chunk_lines
+        line = line + (step % steps_per_block) * lines_per_step
+        start = pl.multiple_of(line * LANES, width)
         index = index_ref[:, pl.ds(start, width)]
         column = index % depth
         upper_part = index // depth
@@ -129,113 +209,55 @@
         mask = row_of == row
         real = jnp.sum(jnp.where(mask, total[:half_rows], 0.0), axis=0, keepdims=True)
         imag = jnp.sum(jnp.where(mask, total[half_rows:], 0.0), axis=0, keepdims=True)
-        for side in range(width // LANES):
-            line = chunk * (width // LANES) + side
+        for side in range(lines_per_step):
             lanes = slice(side * LANES, (side + 1) * LANES)
-            picked[pl.ds(line, 1), :] = real[:, lanes]
-            picked[pl.ds(count // LANES + line, 1), :] = imag[:, lanes]
-
-    for ref in (by_row_ref, by_col_ref):
-        height = ref.shape[1]
-        for block in range(ref.shape[0]):
-            ref[block] = picked[block * height:(block + 1) * height, :].astype(jnp.bfloat16)
-
-
-def transform(product, pw_index, row_count, col_count):
-    points = product.shape[0]
-    count = pw_index.shape[0]
-    lines = 2 * count // LANES
-    tables = [jnp.asarray(table) for table in fourier_tables(points)]
-    depth = 1024
-    whole = pl.BlockSpec(memory_space=pltpu.VMEM)
-    return pl.pallas_call(
-        transform_kernel,
-        out_shape=(
-            jax.ShapeDtypeStruct((row_count, lines // row_count, LANES), jnp.bfloat16),
-            jax.ShapeDtypeStruct((col_count, lines // col_count, LANES), jnp.bfloat16),
-        ),
-        in_specs=[whole] * (2 + len(tables)),
-        out_specs=(whole, whole),
-        scratch_shapes=[
-            pltpu.VMEM((points * points, 2 * points), jnp.float32),
-            pltpu.VMEM((points**3 // depth, depth), jnp.bfloat16),
-            pltpu.VMEM((lines, LANES), jnp.float32),
-        ],
-        name="spectrum",
-    )(product, pw_index.reshape(1, count), *tables)
-
-
-def column_of(row):
-    size = row.shape[1]
-    here = lax.broadcasted_iota(jnp.int32, (size, size), 0)
-    there = lax.broadcasted_iota(jnp.int32, (size, size), 1)
-    return jnp.sum(jnp.where(here == there, row, 0.0), axis=1, keepdims=True)
-
-
-def lookup(indices, table):
-    column = column_of(indices.astype(jnp.float32))
-    slots = lax.broadcasted_iota(jnp.int32, (column.shape[0], table.shape[1]), 1)
-    return jnp.sum(
-        jnp.where(column == slots.astype(jnp.float32), table, 0.0), axis=1, keepdims=True
-    )
-
-
-def exchange_kernel(
-    by_row, by_col, valence_band, conduction_band, valence_energy, conduction_energy, imag_freq,
-    row_panel, col_panel, weights,
-    row_send, row_recv, col_send, col_recv,
-    share_send, share_recv, pass_send, pass_recv, own_sem,
-):
-    rows, cols = row_panel.shape[:2]
-    r, c = lax.axis_index("row"), lax.axis_index("col")
-
-    barrier = pltpu.get_barrier_semaphore()
-
-    def each(count, action):
-        def body(step, carry):
-            action(step)
-            return carry
-
-        lax.fori_loop(1, count, body, 0)
-
-    each(rows, lambda i: pl.semaphore_signal(
-        barrier, inc=1, device_id=(lax.rem(r + i, rows), c), device_id_type=MESH))
-    each(cols, lambda k: pl.semaphore_signal(
-        barrier, inc=1, device_id=(r, lax.rem(c + k, cols)), device_id_type=MESH))
-    pl.semaphore_wait(barrier, rows + cols - 2)
-
-    def remote(source, target, send, recv, device):
-        return pltpu.make_async_remote_copy(
-            src_ref=source, dst_ref=target, send_sem=send, recv_sem=recv,
-            device_id=device, device_id_type=MESH)
-
-    def row_copy(i, source):
-        return remote(
-            by_row.at[lax.rem(r + i, rows)], row_panel.at[source, c],
-            row_send.at[i], row_recv.at[i], (lax.rem(r + i, rows), c))
-
-    def col_copy(k, source):
-        return remote(
-            by_col.at[lax.rem(c + k, cols)], col_panel.at[r, source],
-            col_send.at[k], col_recv.at[k], (r, lax.rem(c + k, cols)))
-
-    def share(i, k, held, source):
-        return remote(
-            held, row_panel.at[lax.rem(r - i + rows, rows), source],
-            share_send.at[i, k], share_recv.at[i, k], (r, lax.rem(c + k, cols)))
-
-    def hand_on(i, source):
-        return remote(
-            col_panel.at[r], col_panel.at[source],
-            pass_send.at[i], pass_recv.at[i], (lax.rem(r + i, rows), c))
-
-    each(rows, lambda i: row_copy(i, r).start())
-    each(cols, lambda k: col_copy(k, c).start())
-    own_row = pltpu.make_async_copy(by_row.at[r], row_panel.at[r, c], own_sem.at[0])
-    own_col = pltpu.make_async_copy(by_col.at[c], col_panel.at[r, c], own_sem.at[1])
-    own_row.start()
-    own_col.start()
-    each(cols, lambda k: share(0, k, by_row.at[r], c).start())
+            picked[pl.ds(line + side, 1), :] = real[:, lanes]
+            picked[pl.ds(count // LANES + line + side, 1), :] = imag[:, lanes]
+
+    def forward(phase):
+        def one(i):
+            source = behind(i)
+            row_copy(phase, i, source).wait_recv()
+            held = row_panel.at[source, c, lines_of(phase)]
+            each(cols, lambda k: share(phase, i, k, held, c).start())
+
+        each(rows, one)
+
+    for phase in range(phases):
+
+        @pl.loop(0, rows // 2 * steps_per_block, unroll=8)
+        def _(step):
+            select(phase, step)
+
+        for block in range(rows):
+            first = block * tall + phase * chunk_lines
+            values = picked[first:first + chunk_lines, :].astype(jnp.bfloat16)
+            by_row[block, phase * chunk_lines:(phase + 1) * chunk_lines, :] = values
+            for at in range(chunk_lines // short):
+                by_col[first // short + at] = picked[
+                    first + at * short:first + (at + 1) * short, :
+                ].astype(jnp.bfloat16)
+        if phase == 0:
+            pl.semaphore_wait(barrier, rows + cols - 2)
+        each(rows, lambda i: row_copy(phase, i, r).start())
+
+        def send_col(k):
+            @pl.when(lax.rem(onward(k) * short // chunk_lines, phases) == phase)
+            def _():
+                col_copy(k, c).start()
+
+        each(cols, send_col)
+        held = by_row.at[r, lines_of(phase)]
+        each(cols, lambda k: share(phase, 0, k, held, c).start())
+        if phase > 0:
+            forward(phase - 1)
+
+    row_panel[r, c] = by_row[r]
+    col_panel[r, c] = by_col[c]
+    each(cols, lambda k: col_copy(k, back(k)).wait_recv())
+    each(rows, lambda i: hand_on(i, r).start())
+    forward(phases - 1)
+
     gap = lookup(conduction_band[...], conduction_energy[...]) - lookup(
         valence_band[...], valence_energy[...]
     )
@@ -243,60 +265,64 @@
     for freq in range(weights.shape[1]):
         omega = imag_freq[:, freq:freq + 1]
         weights[:, freq:freq + 1] = -4.0 * gap / (gap * gap + omega * omega) / root
-    own_row.wait()
-    own_col.wait()
-    each(cols, lambda k: col_copy(k, lax.rem(c - k + cols, cols)).wait_recv())
-    each(rows, lambda i: hand_on(i, r).start())
-
-    def forward(i):
-        source = lax.rem(r - i + rows, rows)
-        row_copy(i, source).wait_recv()
-        each(cols, lambda k: share(i, k, row_panel.at[source, c], c).start())
-
-    each(rows, forward)
-
-    def finish(i, carry):
-        held = row_panel.at[lax.rem(r - i + rows, rows), c]
-
-        def ending(k):
-            share(i, k, held, lax.rem(c - k + cols, cols)).wait_recv()
-            share(i, k, held, c).wait_send()
-
-        each(cols, ending)
-        return carry
-
-    each(rows, lambda i: row_copy(i, r).wait_send())
+
     each(cols, lambda k: col_copy(k, c).wait_send())
 
     def passed(i):
-        hand_on(i, lax.rem(r - i + rows, rows)).wait_recv()
+        hand_on(i, behind(i)).wait_recv()
         hand_on(i, r).wait_send()
 
     each(rows, passed)
-    lax.fori_loop(0, rows, finish, 0)
-
-
-def exchange(by_row, by_col, *bands):
+    for phase in range(phases):
+        each(rows, lambda i: row_copy(phase, i, r).wait_send())
+
+        def finish(i, carry):
+            held = row_panel.at[behind(i), c, lines_of(phase)]
+
+            def ending(k):
+                share(phase, i, k, held, back(k)).wait_recv()
+                share(phase, i, k, held, c).wait_send()
+
+            each(cols, ending)
+            return carry
+
+        lax.fori_loop(0, rows, finish, 0)
+
+
+def transform(product, pw_index, row_count, col_count, *bands):
     bands = [values.reshape(1, -1) for values in bands]
-    rows, cols = by_row.shape[0], by_col.shape[0]
+    points = product.shape[0]
+    count = pw_index.shape[0]
+    lines = 2 * count // LANES
+    tall, short = lines // row_count, lines // col_count
+    phases = 2 if tall % 32 == 0 and (tall // 2) % short == 0 else 1
+    tables = [jnp.asarray(table) for table in fourier_tables(points)]
+    depth = 1024
     whole = pl.BlockSpec(memory_space=pltpu.VMEM)
     dma = pltpu.SemaphoreType.DMA
     return pl.pallas_call(
-        exchange_kernel,
+        transform_kernel,
         out_shape=(
-            jax.ShapeDtypeStruct((rows, cols) + by_row.shape[1:], jnp.bfloat16),
-            jax.ShapeDtypeStruct((rows, cols) + by_col.shape[1:], jnp.bfloat16),
+            jax.ShapeDtypeStruct((row_count, col_count, tall, LANES), jnp.bfloat16),
+            jax.ShapeDtypeStruct((row_count, col_count, short, LANES), jnp.bfloat16),
             jax.ShapeDtypeStruct((bands[0].shape[1], bands[-1].shape[1]), jnp.float32),
         ),
-        in_specs=[whole] * (2 + len(bands)),
+        in_specs=[whole] * (2 + len(tables) + len(bands)),
         out_specs=(whole, whole, whole),
         scratch_shapes=[
-            dma((rows,)), dma((rows,)), dma((cols,)), dma((cols,)),
-            dma((rows, cols)), dma((rows, cols)), dma((rows,)), dma((rows,)), dma((2,)),
+            pltpu.VMEM((points * points, 2 * points), jnp.float32),
+            pltpu.VMEM((points**3 // depth, depth), jnp.bfloat16),
+            pltpu.VMEM((lines, LANES), jnp.float32),
+            pltpu.VMEM((row_count, tall, LANES), jnp.bfloat16),
+            pltpu.VMEM((col_count, short, LANES), jnp.bfloat16),
+            dma((phases, row_count)), dma((phases, row_count)),
+            dma((col_count,)), dma((col_count,)),
+            dma((phases, row_count, col_count)), dma((phases, row_count, col_count)),
+            dma((row_count,)), dma((row_count,)),
         ],
         compiler_params=pltpu.CompilerParams(collective_id=0, has_side_effects=True),
-        name="exchange",
-    )(by_row, by_col, *bands)
+        name="spectrum",
+    )(product, pw_index.reshape(1, count), *tables, *bands)
 
 
 def product_kernel(row_ref, col_ref, weight_ref, out_ref, row_lines, col_lines, left, right, ring, sems):
@@ -390,9 +416,8 @@
     imag_freq,
 ):
     rows, cols = lax.axis_size("row"), lax.axis_size("col")
-    by_row, by_col = transform(pair_products[0], pw_index, rows, cols)
-    row_panel, col_panel, weights = exchange(
-        by_row, by_col,
+    row_panel, col_panel, weights = transform(
+        pair_products[0], pw_index, rows, cols,
         valence_band, conduction_band, valence_energy, conduction_energy, imag_freq,
     )
     return product(row_panel, col_panel, weights)

time: 51.3 us -> 48.6 us (0.947)
  Pallas kernels: 51 us -> 48.4 us
    pallas_call x1 -> x0, Pallas kernels: 15.6 us -> none  [exchange(): pl.pallas_call(exchange_kernel, out_shape=(jax.ShapeDtypeStruct((rows, co...]
    pallas_call x1, Pallas kernels: 12.2 us -> 25.3 us  [transform(): pl.pallas_call(transform_kernel, out_shape=(jax.ShapeDtypeStruct((row_cou...]
where the time goes in v3:
time: 48.6 us; the launch traced here: 48.4 us
  Pallas kernels  48.4 us (100%)
    pallas_call x1, Pallas kernels, transform(): pl.pallas_call(transform_kernel, out_shape=(jax.ShapeDtypeStruct((row_cou...  25.3 us
    pallas_call x1, Pallas kernels, product(): pl.pallas_call(product_kernel, out_shape=jax.ShapeDtypeStruct((freq_count...  23.2 us

profile of v3, /device:TPU:0, one launch (start us, length us, event | category | flops | bytes accessed | tf_op | source)
XLA Modules:
  0.0 48.4 jit_solution(14579655733209129906)
XLA Ops:
  0.0 25.3 %spectrum.1 = (bf16[4,8,32,128]{3,2,1,0:T(8,128)(2,1)}, bf16[4,8,16,128]{3,2,1,0:T(8,128)(2,1)}, f32[32,2]{1,0:T(8,128)}) custom-call(bf16[64,64,64]{2,1,0:T(8,128)(2,1)} %bitcast.9, s32[1,8192]{1,0:T(1,128)} %bitcast.12, bf16[128,128]{1,0:T(8,128)(2,1)} %constant.6.clone.z_ref, bf16[128,192]{1,0:T(8,128)(2,1)} %constant.7.clone.y_ref, ...), custom_call_target="tpu_custom_call" | custom-call | tf_op jit(solution)/shard_map/spectrum/pallas_call | solution.py:303
  25.3 23.2 %product.1 = f32[2,4096,2048]{2,1,0:T(8,128)} custom-call(bf16[32,32,128]{2,1,0:T(8,128)(2,1)} %bitcast.10, bf16[32,16,128]{2,1,0:T(8,128)(2,1)} %bitcast.11, f32[32,2]{1,0:T(8,128)} %get-tuple-element.10.weight_ref), custom_call_target="tpu_custom_call" | custom-call | tf_op jit(solution)/shard_map/product/pallas_call | solution.py:394

commit v4 on v3

--- a/solution.py
+++ b/solution.py
@@ -223,6 +223,14 @@
 
         each(rows, one)
 
+    def phase_of(block):
+        return lax.rem(block * short // chunk_lines, phases)
+
+    def pass_columns():
+        col_panel[r, c] = by_col[c]
+        each(cols, lambda k: col_copy(k, back(k)).wait_recv())
+        each(rows, lambda i: hand_on(i, r).start())
+
     for phase in range(phases):
 
         @pl.loop(0, rows // 2 * steps_per_block, unroll=8)
@@ -242,20 +250,20 @@
         each(rows, lambda i: row_copy(phase, i, r).start())
 
         def send_col(k):
-            @pl.when(lax.rem(onward(k) * short // chunk_lines, phases) == phase)
+            @pl.when(phase_of(onward(k)) == phase)
             def _():
                 col_copy(k, c).start()
 
         each(cols, send_col)
+        if phase > 0:
+            pl.when(phase_of(c) == phase - 1)(pass_columns)
         held = by_row.at[r, lines_of(phase)]
         each(cols, lambda k: share(phase, 0, k, held, c).start())
         if phase > 0:
             forward(phase - 1)
 
     row_panel[r, c] = by_row[r]
-    col_panel[r, c] = by_col[c]
-    each(cols, lambda k: col_copy(k, back(k)).wait_recv())
-    each(rows, lambda i: hand_on(i, r).start())
+    pl.when(phase_of(c) == phases - 1)(pass_columns)
     forward(phases - 1)
 
     gap = lookup(conduction_band[...], conduction_energy[...]) - lookup(
@@ -336,15 +344,13 @@
             lines[...] = ref[...].astype(jnp.float32).reshape(lines.shape)
         else:
             blocks = ref.shape[1] // LANES
-        for block in range(blocks):
+        for block in range(0 if is_left else blocks):
             lanes = slice(block * LANES, (block + 1) * LANES)
             if len(ref.shape) == 3:
                 values = lines[pl.ds(block, pairs, stride=blocks), :]
             else:
                 values = ref[:, lanes].astype(jnp.float32)
-            if is_left:
-                left[lanes, :] = values.T.astype(jnp.bfloat16)
-            else:
+            if not is_left:
                 for freq in range(freq_count):
                     right[freq, :, lanes] = (
                         values * weight_ref[:, freq:freq + 1]
@@ -358,7 +364,15 @@
 
     @pl.loop(0, steps)
     def _(step):
-        panel = left[pl.ds(pl.multiple_of(step * height, height), height), :]
+        for part in range(height // LANES):
+            block = step * (height // LANES) + part
+            if len(row_ref.shape) == 3:
+                values = row_lines[pl.ds(block, pairs, stride=row_ref.shape[1]), :]
+            else:
+                values = row_ref[:, pl.ds(pl.multiple_of(block * LANES, LANES), LANES)]
+                values = values.astype(jnp.float32)
+            left[part * LANES:(part + 1) * LANES, :] = values.T.astype(jnp.bfloat16)
+        panel = left[...]
         for freq in range(freq_count):
             unit = step * freq_count + freq
             slot = lax.rem(unit, slots)
@@ -397,7 +411,7 @@
         in_specs=[whole, whole, whole],
         out_specs=pl.BlockSpec(memory_space=pl.ANY),
         scratch_shapes=lines + [
-            pltpu.VMEM((row_width, pairs), jnp.bfloat16),
+            pltpu.VMEM((block, pairs), jnp.bfloat16),
             pltpu.VMEM((freq_count, pairs, col_width), jnp.bfloat16),
             pltpu.VMEM((slots, block, col_width), jnp.float32),
             pltpu.SemaphoreType.DMA((slots,)),

time: 48.6 us -> 48.2 us (level)
  no operation moved by 1% of the time
where the time goes in v4:
time: 48.2 us; the launch traced here: 48 us
  Pallas kernels  48 us (100%)
    pallas_call x1, Pallas kernels, transform(): pl.pallas_call(transform_kernel, out_shape=(jax.ShapeDtypeStruct((row_cou...  25.2 us
    pallas_call x1, Pallas kernels, product(): pl.pallas_call(product_kernel, out_shape=jax.ShapeDtypeStruct((freq_count...  22.9 us

profile of v4, /device:TPU:0, one launch (start us, length us, event | category | flops | bytes accessed | tf_op | source)
XLA Modules:
  0.0 48.0 jit_solution(18194545288201175286)
XLA Ops:
  0.0 25.2 %spectrum.1 = (bf16[4,8,32,128]{3,2,1,0:T(8,128)(2,1)}, bf16[4,8,16,128]{3,2,1,0:T(8,128)(2,1)}, f32[32,2]{1,0:T(8,128)}) custom-call(bf16[64,64,64]{2,1,0:T(8,128)(2,1)} %bitcast.9, s32[1,8192]{1,0:T(1,128)} %bitcast.12, bf16[128,128]{1,0:T(8,128)(2,1)} %constant.6.clone.z_ref, bf16[128,192]{1,0:T(8,128)(2,1)} %constant.7.clone.y_ref, ...), custom_call_target="tpu_custom_call" | custom-call | tf_op jit(solution)/shard_map/spectrum/pallas_call | solution.py:311
  25.2 22.9 %product.1 = f32[2,4096,2048]{2,1,0:T(8,128)} custom-call(bf16[32,32,128]{2,1,0:T(8,128)(2,1)} %bitcast.10, bf16[32,16,128]{2,1,0:T(8,128)(2,1)} %bitcast.11, f32[32,2]{1,0:T(8,128)} %get-tuple-element.10.weight_ref), custom_call_target="tpu_custom_call" | custom-call | tf_op jit(solution)/shard_map/product/pallas_call | solution.py:408
